TPU v7x, 256 devices: a whole 4x4x8 slice. The times are simulated.
256 devices in a mesh: seq: 16 (over y, z_hi, core), mp: 16 (over z_lo, x).
Axes of the slice: x: 4, y: 4, z: 8 (z_hi: 2, z_lo: 4; z = z_hi * 4 + z_lo), core: 2. Of those that a mesh axis runs over, the one named last changes fastest.
Arguments:
- hidden_in: bfloat16 [2048, 2048], P('seq'), may hold values from -0.59765625 to 0.59765625
- input_gain: float32 [2048], replicated, may hold values from 0.25 to 1.75
- w_query: bfloat16 [2048, 2048], P(None, 'mp'), may hold values from -0.125 to 0.125
- key_value_weight: bfloat16 [2048, 4096], P(None, 'mp'), may hold values from -1 to 1, as said below
- query_gain: float32 [128], replicated, may hold values from 0.25 to 1.75
- key_gain: float32 [128], replicated, may hold values from 0.25 to 1.75
- w_out: bfloat16 [2048, 2048], P('mp'), may hold values from -0.125 to 0.125
- post_gain: float32 [2048], replicated, may hold values from 0.25 to 1.75
- w_gate: bfloat16 [2048, 6144], P(None, 'mp'), may hold values from -0.125 to 0.125
- w_up: bfloat16 [2048, 6144], P(None, 'mp'), may hold values from -0.125 to 0.125
- w_down: bfloat16 [6144, 2048], P('mp'), may hold values from -0.078125 to 0.078125
- prefix_slot_cache: bfloat16 [32, 256, 8, 256], P('seq'), may hold values from -240 to 240, as said below
- block_table: int32 [32], replicated, may hold values from 0 to 31, each once
- request_prefix: int32 [32], replicated, may hold values from 0 to 3
- suffix_lengths: int32 [32], replicated, may hold values from 1 to 256, 2048 in all
Outputs:
- hidden_out: bfloat16 [2048, 2048], P('seq', 'mp')
- suffix_key_values: bfloat16 [2048, 2048], P('seq', 'mp')
Inputs may be any that keep to these rules, and one draw needn't show every extreme that they name: block_table[p * 8 + i] is the slot holding block i of prefix p; every slot appears once. `suffix_lengths`: the lengths add up to 2048 and the longest is exactly 256. `prefix_slot_cache`: per slot, position and key-value head: a key in the first 128 entries, a value in the last 128. `key_value_weight`: columns of key-value head k: 2 equal blocks of 256, starting at k * 2 * 2 * 128.
All inputs are finite; a program needn't handle non-finite values.
Results may differ from a plain program's by a relative error of at most 0.025.
The roundings to bfloat16 on the way count: a program that leaves them out, or rounds other values in their place, can miss the bound.
Values may be sent and summed in bfloat16 or wider, within the bound.
A program may use at most 64 MiB of HBM per device.

v0:
```python
import math
import jax
import jax.numpy as jnp
from jax import lax
from jax.sharding import PartitionSpec as P

QUERY_HEADS = 16
KEY_VALUE_HEADS = 8
HEAD_WIDTH = 128
N_PREFIX = 4
EPSILON = 1e-06
THETA = 1000000.0
NEGATIVE_FLOOR = -1e30


def token_tables(request_prefix, suffix_lengths, positions, prefix_length):
    request_ends = jnp.cumsum(suffix_lengths)
    starts = request_ends - suffix_lengths
    inside = (
        (positions[:, None] >= starts[None, :]) & (positions[:, None] < request_ends[None, :])
    ).astype(jnp.int32)
    request_ids = jnp.arange(suffix_lengths.shape[0], dtype=jnp.int32)
    request_of = jnp.sum(inside * request_ids[None, :], axis=1)
    start_of = jnp.sum(inside * starts[None, :], axis=1)
    prefix_of = jnp.sum(inside * request_prefix[None, :], axis=1)
    rotary_pos = prefix_length + positions - start_of
    return (request_of, prefix_of, rotary_pos)


def row_norm(values, gain):
    return values * lax.rsqrt(jnp.mean(values * values, axis=-1, keepdims=True) + EPSILON) * gain


def head_norm(values, gain):
    return values * lax.rsqrt(jnp.mean(values * values, axis=-1, keepdims=True) + EPSILON) * gain


def rotate(values, rotary_pos):
    half_dim = values.shape[-1] // 2
    freq_ids = jnp.arange(half_dim).astype(jnp.float32)
    inverse = jnp.exp(freq_ids * (-2.0 * math.log(THETA) / values.shape[-1]))
    angles = rotary_pos.astype(jnp.float32)[:, None] * inverse[None, :]
    cosine = jnp.cos(angles)[:, None, :]
    sine_part = jnp.sin(angles)[:, None, :]
    first_half = values[..., :half_dim]
    second_half = values[..., half_dim:]
    return jnp.concatenate(
        [
            first_half * cosine - second_half * sine_part,
            second_half * cosine + first_half * sine_part,
        ],
        axis=-1,
    )


def allowed_keys(query_req, query_pre, query_pos, key_pre, key_req, key_pos):
    same_prefix = key_pre[None, :] == query_pre[:, None]
    same_request = (key_req[None, :] == query_req[:, None]) & (
        key_pos[None, :] <= query_pos[:, None]
    )
    return same_prefix | same_request


def group_partial(query_rows_all, allowed, key_row_block, value_row_block):
    scaling = 1.0 / math.sqrt(query_rows_all.shape[-1])
    scores = (
        jnp.einsum(
            "nkgd,mkd->nkgm", query_rows_all, key_row_block, preferred_element_type=jnp.float32
        )
        * scaling
    )
    allowed_full = allowed[:, None, None, :]
    scores = jnp.where(allowed_full, scores, NEGATIVE_FLOOR)
    highest_score = jnp.max(scores, axis=-1)
    weights = jnp.where(allowed_full, jnp.exp(scores - highest_score[..., None]), 0.0)
    total_weight = jnp.sum(weights, axis=-1)
    rounded = weights.astype(jnp.bfloat16)
    summed = jnp.einsum(
        "nkgm,mkd->nkgd", rounded, value_row_block, preferred_element_type=jnp.float32
    )
    layer_output = (summed / jnp.maximum(total_weight, 1.0)[..., None]).astype(jnp.bfloat16)
    return (highest_score, total_weight, layer_output)


def tile_partials(query_rows, query_req, query_pre, query_pos, bundle, tile_rows):
    key_row_block, value_row_block, key_pre, key_req, key_pos = bundle
    token_count = query_rows.shape[0]
    tile_count = token_count // tile_rows
    shaped = (
        query_rows.reshape((tile_count, tile_rows) + query_rows.shape[1:]),
        query_req.reshape(tile_count, tile_rows),
        query_pre.reshape(tile_count, tile_rows),
        query_pos.reshape(tile_count, tile_rows),
    )

    def one_tile(members):
        tile_queries, tile_req, tile_pre, tile_pos = members
        allowed = allowed_keys(tile_req, tile_pre, tile_pos, key_pre, key_req, key_pos)

        def computed(unused):
            return group_partial(tile_queries, allowed, key_row_block, value_row_block)

        def skipped(unused):
            stats_shape = tile_queries.shape[:-1]
            return (
                jnp.full(stats_shape, NEGATIVE_FLOOR, jnp.float32),
                jnp.zeros(stats_shape, jnp.float32),
                jnp.zeros(tile_queries.shape, jnp.bfloat16),
            )

        return lax.cond(jnp.any(allowed), computed, skipped, 0)

    highest_score, total_weight, layer_output = lax.map(one_tile, shaped)
    stats_shape = (token_count,) + query_rows.shape[1:-1]
    return (
        highest_score.reshape(stats_shape),
        total_weight.reshape(stats_shape),
        layer_output.reshape(query_rows.shape),
    )


def local(
    hidden_in,
    input_gain,
    w_query,
    key_value_weight,
    query_gain,
    key_gain,
    w_out,
    post_gain,
    w_gate,
    w_up,
    w_down,
    prefix_slot_cache,
    block_table,
    request_prefix,
    suffix_lengths,
):
    seq_count = lax.axis_size("seq")
    model_count = lax.axis_size("mp")
    my_seq = lax.axis_index("seq")
    my_model = lax.axis_index("mp")
    rows_here = hidden_in.shape[0]
    local_heads = w_query.shape[1] // HEAD_WIDTH
    group_width = QUERY_HEADS // KEY_VALUE_HEADS
    shared_heads = max(1, local_heads // group_width)
    query_per_head = local_heads // shared_heads
    pair_width = 2 * HEAD_WIDTH
    first_shared = my_model * local_heads // group_width
    blocks_here = prefix_slot_cache.shape[0]
    block_rows = prefix_slot_cache.shape[1]
    cache_extent = blocks_here * block_rows
    slot_total = blocks_here * seq_count
    prefix_length = slot_total // N_PREFIX * block_rows
    all_tokens = rows_here * seq_count
    hidden_f32 = hidden_in.astype(jnp.float32)
    normed = row_norm(hidden_f32, input_gain).astype(jnp.bfloat16)
    own_pos = my_seq * rows_here + jnp.arange(rows_here, dtype=jnp.int32)
    own_req, own_pre, own_rot = token_tables(request_prefix, suffix_lengths, own_pos, prefix_length)
    query_raw = jnp.dot(normed, w_query, preferred_element_type=jnp.float32).reshape(
        rows_here, local_heads, HEAD_WIDTH
    )
    query_rows_all = rotate(head_norm(query_raw, query_gain), own_rot).astype(jnp.bfloat16)
    pair_block = jnp.dot(normed, key_value_weight, preferred_element_type=jnp.float32).astype(
        jnp.bfloat16
    )
    share_ratio = max(1, group_width // local_heads)
    pair_split = pair_block.reshape(rows_here, shared_heads, 2, HEAD_WIDTH)
    key_row_block = rotate(
        head_norm(pair_split[:, :, 0].astype(jnp.float32), key_gain), own_rot
    ).astype(jnp.bfloat16)
    pairs_mine = jnp.stack([key_row_block, pair_split[:, :, 1]], axis=2).reshape(
        rows_here, shared_heads, pair_width
    )
    cache_cols = shared_heads * pair_width // share_ratio
    suffix_key_values = lax.dynamic_slice_in_dim(
        pairs_mine.reshape(rows_here, shared_heads * pair_width),
        my_model % share_ratio * cache_cols,
        cache_cols,
        1,
    )
    slot_ids = jnp.arange(slot_total, dtype=jnp.int32)
    owner_hits = (block_table[:, None] == slot_ids[None, :]).astype(jnp.int32)
    slot_prefix = jnp.sum(owner_hits * (slot_ids // (slot_total // N_PREFIX))[:, None], axis=0)
    cache_mine = lax.dynamic_slice_in_dim(prefix_slot_cache, first_shared, shared_heads, 2).reshape(
        cache_extent, shared_heads, pair_width
    )
    query_all = lax.all_gather(
        query_rows_all.reshape(rows_here, local_heads * HEAD_WIDTH), "seq", axis=0, tiled=True
    )
    query_all = query_all.reshape(all_tokens, shared_heads, query_per_head, HEAD_WIDTH)
    all_pos = jnp.arange(all_tokens, dtype=jnp.int32)
    all_req, all_pre, _ = token_tables(request_prefix, suffix_lengths, all_pos, prefix_length)
    group_pre = jnp.repeat(
        lax.dynamic_slice_in_dim(slot_prefix, my_seq * blocks_here, blocks_here), block_rows
    )
    key_positions = my_seq * rows_here + jnp.arange(rows_here, dtype=jnp.int32)
    group_req, _, _ = token_tables(request_prefix, suffix_lengths, key_positions, prefix_length)
    all_keys = jnp.concatenate([cache_mine[..., :HEAD_WIDTH], pairs_mine[..., :HEAD_WIDTH]], axis=0)
    all_values = jnp.concatenate(
        [cache_mine[..., HEAD_WIDTH:], pairs_mine[..., HEAD_WIDTH:]], axis=0
    )
    key_pre = jnp.concatenate([group_pre, jnp.full((rows_here,), -1, jnp.int32)])
    key_req = jnp.concatenate([jnp.full((cache_extent,), -1, jnp.int32), group_req])
    key_pos = jnp.concatenate([jnp.zeros((cache_extent,), jnp.int32), key_positions])
    bundle = (all_keys, all_values, key_pre, key_req, key_pos)
    highest_score, total_weight, layer_output = tile_partials(
        query_all, all_req, all_pre, all_pos, bundle, min(512, all_tokens)
    )
    highest_score = highest_score.reshape(seq_count, rows_here, shared_heads, query_per_head)
    total_weight = total_weight.reshape(seq_count, rows_here, shared_heads, query_per_head)
    layer_output = layer_output.reshape(
        seq_count, rows_here, shared_heads, query_per_head, HEAD_WIDTH
    )
    widened = lax.optimization_barrier(layer_output).astype(jnp.float32)
    result_back, peak_back, total_back = (
        lax.all_to_all(widened, "seq", split_axis=0, concat_axis=0, tiled=True),
        lax.all_to_all(highest_score, "seq", split_axis=0, concat_axis=0, tiled=True),
        lax.all_to_all(total_weight, "seq", split_axis=0, concat_axis=0, tiled=True),
    )
    best_score = jnp.max(peak_back, axis=0)
    scaling = total_back * jnp.exp(peak_back - best_score[None])
    attended = (
        jnp.sum(scaling[..., None] * result_back, axis=0) / jnp.sum(scaling, axis=0)[..., None]
    )
    attended = attended.astype(jnp.bfloat16).reshape(rows_here, local_heads * HEAD_WIDTH)
    partial_out = jnp.dot(attended, w_out, preferred_element_type=jnp.float32)
    column_count = hidden_in.shape[1] // model_count
    summed = lax.psum(partial_out.astype(jnp.bfloat16), "mp").astype(jnp.float32)
    residual = (hidden_f32 + summed).astype(jnp.bfloat16)
    residual_cols = lax.dynamic_slice_in_dim(residual, my_model * column_count, column_count, 1)
    post_normed = row_norm(residual.astype(jnp.float32), post_gain).astype(jnp.bfloat16)
    gate_terms = jnp.dot(post_normed, w_gate, preferred_element_type=jnp.float32)
    up_terms = jnp.dot(post_normed, w_up, preferred_element_type=jnp.float32)
    middle = (jax.nn.silu(gate_terms) * up_terms).astype(jnp.bfloat16)
    down_terms = jnp.dot(middle, w_down, preferred_element_type=jnp.float32)
    hidden_part = lax.psum_scatter(
        down_terms.astype(jnp.bfloat16), "mp", scatter_dimension=1, tiled=True
    ).astype(jnp.float32)
    hidden_out = (residual_cols.astype(jnp.float32) + hidden_part).astype(jnp.bfloat16)
    return (hidden_out, suffix_key_values)


def solution(mesh):
    in_specs = (
        P("seq", None),
        P(),
        P(None, "mp"),
        P(None, "mp"),
        P(),
        P(),
        P("mp", None),
        P(),
        P(None, "mp"),
        P(None, "mp"),
        P("mp", None),
        P("seq", None, None, None),
        P(),
        P(),
        P(),
    )
    out_specs = (P("seq", "mp"), P("seq", "mp"))
    return jax.shard_map(local, mesh=mesh, in_specs=in_specs, out_specs=out_specs, check_vma=False)
```

profile of v0, /device:TPU:8, one launch (start us, length us, event | category | flops | bytes accessed | tf_op | source)
XLA Modules:
  0.0 402.8 jit_solution(13331135312913714287)
XLA Ops:
  7.3 1.4 fusion.20
  8.7 1.8 convolution_convert_fusion.2
  10.5 0.1 copy.47
  11.1 0.1 reduce.10
  11.4 0.2 select_reduce_fusion
  11.7 0.4 multiply_reduce_fusion.1
  12.3 0.2 fusion.58
  12.6 0.1 copy.59
  12.7 0.1 copy.58
  12.8 33.7 %all_gather.3 = bf16[2048,128]{0,1:T(8,128)(2,1)S(1)} all-gather(bf16[128,128]{0,1:T(8,128)(2,1)S(1)} %pad_maximum_fusion.3), channel_id=1, replica_groups=mesh['seq'=16,'mp'=16] {'seq'}, dimensions={0}, use_global_device_ids=true | all-gather | bytes 557056 | tf_op jit(solution)/shard_map/all_gather | solution.py:188
  46.5 0.3 copy.54
  46.8 0.5 constant_dynamic-slice_fusion.3
  47.5 33.2 %while.14 = (s32[]{:T(128)}, f32[4,512,1,1]{1,3,2,0:T(1,128)S(1)}, f32[4,512,1,1]{1,3,2,0:T(1,128)}, bf16[4,512,1,1,128]{4,1,3,2,0:T(8,128)(2,1)}, s32[640]{0:T(...) while((s32[]{:T(128)}, f32[4,512,1,1]{1,3,2,0:T(1,128)S(1)}, ...), condition=%wide.region_15.16_spmd, body=%wide.region_9.15_spmd.sunk | while | flops 172817920 | bytes 6144739 | solution.py:113
  47.5 1.0 fusion.76
  49.2 4.6 %conditional.2 = (f32[1,512,1,1]{1,3,2,0:T(1,128)}, f32[1,512,1,1]{1,3,2,0:T(1,128)}, bf16[1,512,1,1,128]{4,1,3,2,0:T(8,128)(2,1)S(1)}) conditional(s32[]{:T(128)} %convert_element_type.195, () %tuple.64, (pred[512,640]{1,0:T(32,128)(4,1)S(1)}, bf16[4,512,1,1,128]{4,1,3,2,0:T(8,128)(2,1)S(1)}, s32[]{:T(128)}, bf16[640,1,128]{2,0,1:T(8,128)(2,1)S(1)}, ...), branch_computations={%region_11.11_spmd, %region_12.14_spmd} | conditional | flops 170851840 | bytes 5519388 | solution.py:111
  49.2 1.1 fusion.66
  50.3 1.7 fusion.5
  52.0 0.7 broadcast_maximum_fusion
  52.7 1.1 fusion.3
  53.8 1.3 constant_dynamic-update-slice_fusion.5
  55.1 0.7 constant_dynamic-update-slice_fusion.6
  55.8 1.0 fusion.76
  57.5 4.6 %conditional.2 = (f32[1,512,1,1]{1,3,2,0:T(1,128)}, f32[1,512,1,1]{1,3,2,0:T(1,128)}, bf16[1,512,1,1,128]{4,1,3,2,0:T(8,128)(2,1)S(1)}) conditional(s32[]{:T(128)} %convert_element_type.195, () %tuple.64, (pred[512,640]{1,0:T(32,128)(4,1)S(1)}, bf16[4,512,1,1,128]{4,1,3,2,0:T(8,128)(2,1)S(1)}, s32[]{:T(128)}, bf16[640,1,128]{2,0,1:T(8,128)(2,1)S(1)}, ...), branch_computations={%region_11.11_spmd, %region_12.14_spmd} | conditional | flops 170851840 | bytes 5519388 | solution.py:111
  57.5 1.1 fusion.66
  58.6 1.7 fusion.5
  60.3 0.7 broadcast_maximum_fusion
  61.0 1.1 fusion.3
  62.1 1.3 constant_dynamic-update-slice_fusion.5
  63.4 0.7 constant_dynamic-update-slice_fusion.6
  64.1 1.0 fusion.76
  65.8 4.6 %conditional.2 = (f32[1,512,1,1]{1,3,2,0:T(1,128)}, f32[1,512,1,1]{1,3,2,0:T(1,128)}, bf16[1,512,1,1,128]{4,1,3,2,0:T(8,128)(2,1)S(1)}) conditional(s32[]{:T(128)} %convert_element_type.195, () %tuple.64, (pred[512,640]{1,0:T(32,128)(4,1)S(1)}, bf16[4,512,1,1,128]{4,1,3,2,0:T(8,128)(2,1)S(1)}, s32[]{:T(128)}, bf16[640,1,128]{2,0,1:T(8,128)(2,1)S(1)}, ...), branch_computations={%region_11.11_spmd, %region_12.14_spmd} | conditional | flops 170851840 | bytes 5519388 | solution.py:111
  65.8 1.1 fusion.66
  66.9 1.7 fusion.5
  68.6 0.7 broadcast_maximum_fusion
  69.3 1.1 fusion.3
  70.4 1.3 constant_dynamic-update-slice_fusion.5
  71.7 0.7 constant_dynamic-update-slice_fusion.6
  72.4 1.0 fusion.76
  74.1 4.6 %conditional.2 = (f32[1,512,1,1]{1,3,2,0:T(1,128)}, f32[1,512,1,1]{1,3,2,0:T(1,128)}, bf16[1,512,1,1,128]{4,1,3,2,0:T(8,128)(2,1)S(1)}) conditional(s32[]{:T(128)} %convert_element_type.195, () %tuple.64, (pred[512,640]{1,0:T(32,128)(4,1)S(1)}, bf16[4,512,1,1,128]{4,1,3,2,0:T(8,128)(2,1)S(1)}, s32[]{:T(128)}, bf16[640,1,128]{2,0,1:T(8,128)(2,1)S(1)}, ...), branch_computations={%region_11.11_spmd, %region_12.14_spmd} | conditional | flops 170851840 | bytes 5519388 | solution.py:111
  74.1 1.1 fusion.66
  75.1 1.7 fusion.5
  76.9 0.7 broadcast_maximum_fusion
  77.6 1.1 fusion.3
  78.7 1.3 constant_dynamic-update-slice_fusion.5
  80.0 0.7 constant_dynamic-update-slice_fusion.6
  80.6 13.7 %all_to_all.15 = f32[16,128,1,1]{1,3,2,0:T(1,128)S(1)} all-to-all(f32[16,128,1,1]{1,3,2,0:T(1,128)S(1)} %bitcast.115), channel_id=1, replica_groups=mesh['seq'=16,'mp'=16] {'seq'}, dimensions={0} | all-to-all | bytes 16384 | tf_op jit(solution)/shard_map/all_to_all | solution.py:218
  94.3 4.7 %all-to-all-start = ((f32[16,128,1,1]{1,3,2,0:T(1,128)}), f32[16,128,1,1]{1,3,2,0:T(1,128)S(1)}, u32[]{:S(2)}, u32[]{:S(2)}) async-start(f32[16,128,1,1]{1,3,2,0:T(1,128)} %bitcast.29), calls=%async_computation | async-start | bytes 16384 | tf_op jit(solution)/shard_map/all_to_all | solution.py:219
  99.0 2.1 convert_element_type.121
  101.2 6.5 %all-to-all-done = f32[16,128,1,1]{1,3,2,0:T(1,128)S(1)} async-done(((f32[16,128,1,1]{1,3,2,0:T(1,128)}), f32[16,128,1,1]{1,3,2,0:T(1,128)S(1)}, u32[]{:S(2)}, u32[]{:S(2)}) %all-to-all-start) | async-done | bytes 8224 | tf_op jit(solution)/shard_map/all_to_all | solution.py:219
  107.6 4.9 %all-to-all-start.2 = ((f32[16,128,1,1,128]{4,1,3,2,0:T(8,128)}), f32[16,128,1,1,128]{4,1,3,2,0:T(8,128)S(1)}, u32[]{:S(2)}, u32[]{:S(2)}) async-start(f32[16,128,1,1,128]{4,1,3,2,0:T(8,128)} %convert_element_type.121), calls=%async_computation.2 | async-start | bytes 2097152 | tf_op jit(solution)/shard_map/all_to_all | solution.py:217
  112.6 23.0 %all-to-all-done.2 = f32[16,128,1,1,128]{4,1,3,2,0:T(8,128)S(1)} async-done(((f32[16,128,1,1,128]{4,1,3,2,0:T(8,128)}), f32[16,128,1,1,128]{4,1,3,2,0:T(8,128)S(1)}, u32[]{:S(2)}, u32[]{:S(2)}) %all-to-all-start.2) | async-done | bytes 1048608 | tf_op jit(solution)/shard_map/all_to_all | solution.py:217
  135.6 0.3 multiply_reduce_fusion
  136.0 0.7 copy-done.3
  136.7 1.2 convolution_convert_fusion.1
  137.9 167.1 %all-reduce.5.cloned.1.call-done = bf16[128,2048]{1,0:T(8,128)(2,1)} async-done(((bf16[128,2048]{1,0:T(8,128)(2,1)}), bf16[128,2048]{1,0:T(8,128)(2,1)}) %all-reduce.5.cloned.1.call-update) | async-done | bytes 524304 | tf_op jit(solution)/shard_map/psum | solution.py:229
  305.0 1.4 fusion.17
  306.4 0.1 copy-done.8
  306.6 0.5 fusion.32
  307.0 2.8 convolution_convert_fusion
  309.8 1.0 copy.55
  310.9 0.7 copy.60
  311.6 82.8 %reduce-scatter.4.cloned.1.call-done = bf16[128,128]{1,0:T(8,128)(2,1)} async-done(((bf16[2048,128]{1,0:T(8,128)(2,1)}), bf16[128,128]{1,0:T(8,128)(2,1)}) %reduce-scatter.4.cloned.1.call-update) | async-done | bytes 32784
  394.4 0.9 copy.56
  395.3 0.6 add_convert_fusion
  (78 shorter events, 1.3 us)
Async XLA Ops:
  7.2 39.6 %copy-start = (bf16[2,256,8,256]{3,2,1,0:T(8,128)(2,1)S(1)}, bf16[2,256,8,256]{3,2,1,0:T(8,128)(2,1)}, u32[]{:S(2)}) copy-start(bf16[2,256,8,256]{3,2,1,0:T(8,128)(2,1)} %param.30) | copy-start | bytes 6291460
  7.2 3.5 copy-start.12
  7.3 3.7 copy-start.6
  7.3 4.1 %copy-start.7 = (s32[32]{0:T(128)S(1)}, s32[32]{0:T(128)}, u32[]{:S(2)}) copy-start(s32[32]{0:T(128)} %param.32) | copy-start | bytes 388
  7.3 4.4 %copy-start.1 = (bf16[128,2048]{1,0:T(8,128)(2,1)S(1)}, bf16[128,2048]{1,0:T(8,128)(2,1)}, u32[]{:S(2)}) copy-start(bf16[128,2048]{1,0:T(8,128)(2,1)} %param.19) | copy-start | bytes 1572868
  7.3 4.4 %copy-start.9 = (bf16[2048,128]{1,0:T(8,128)(2,1)S(1)}, bf16[2048,128]{1,0:T(8,128)(2,1)}, u32[]{:S(2)}) copy-start(bf16[2048,128]{1,0:T(8,128)(2,1)} %param.21) | copy-start | bytes 1572868
  7.3 4.4 %copy-start.10 = (f32[2048]{0:T(1024)S(1)}, f32[2048]{0:T(1024)}, u32[]{:S(2)}) copy-start(f32[2048]{0:T(1024)} %param.20) | copy-start | bytes 24580
  10.5 1.6 copy-start.4
  10.5 1.7 copy-start.5
  94.3 13.3 %all-to-all-start = ((f32[16,128,1,1]{1,3,2,0:T(1,128)}), f32[16,128,1,1]{1,3,2,0:T(1,128)S(1)}, u32[]{:S(2)}, u32[]{:S(2)}) async-start(f32[16,128,1,1]{1,3,2,0:T(1,128)} %bitcast.29), calls=%async_computation | async-start | bytes 16384 | tf_op jit(solution)/shard_map/all_to_all | solution.py:219
  107.6 28.0 %all-to-all-start.2 = ((f32[16,128,1,1,128]{4,1,3,2,0:T(8,128)}), f32[16,128,1,1,128]{4,1,3,2,0:T(8,128)S(1)}, u32[]{:S(2)}, u32[]{:S(2)}) async-start(f32[16,128,1,1,128]{4,1,3,2,0:T(8,128)} %convert_element_type.121), calls=%async_computation.2 | async-start | bytes 2097152 | tf_op jit(solution)/shard_map/all_to_all | solution.py:217
  112.5 192.5 %all-reduce.5.cloned.1.call-start = ((), (), s32[]{:S(2)}) async-start(), calls=%async_computation.4 | async-start | bytes 1048576 | tf_op jit(solution)/shard_map/psum | solution.py:229
  135.6 1.0 copy-start.3
  136.0 169.0 %copy-start.2 = (bf16[128,2048]{1,0:T(8,128)(2,1)S(1)}, bf16[128,2048]{1,0:T(8,128)(2,1)}, u32[]{:S(2)}) copy-start(bf16[128,2048]{1,0:T(8,128)(2,1)} %param.19) | copy-start | bytes 1572868
  137.8 168.6 %copy-start.11 = (f32[2048]{0:T(1024)S(1)}, f32[2048]{0:T(1024)}, u32[]{:S(2)}) copy-start(f32[2048]{0:T(1024)} %param.26) | copy-start | bytes 24580
  137.9 256.6 %reduce-scatter.4.cloned.1.call-start = ((), (), s32[]{:S(2)}) async-start(), calls=%async_computation.5 | async-start | bytes 557056
  305.0 1.6 copy-start.8
Sparse Core Ops, SparseCore 0:
  138.0 166.9 all-reduce.4
  311.0 83.4 reduce-scatter.3
where the time goes:
time: 404 us; the launch traced here: 403 us
  waiting for transfers between devices  279 us (69%)
  blocking collectives  47.4 us (12%)
  other arithmetic  20.9 us (5%)
  matrix products  15.3 us (4%)
  between operations  14.5 us (4%)
  local copies, waits for them, and re-layouts  12.8 us (3%)
  starting transfers between devices  9.69 us (2%)
    psum x1, waiting for transfers between devices, local(): lax.psum(partial_out.astype(jnp.bfloat16), 'mp').astype(jnp.float32)  167 us
    unnamed x3, waiting for transfers between devices  82.9 us
    all_gather x1, blocking collectives, local(): lax.all_gather(query_rows_all.reshape(rows_here, local_heads * HEAD_WIDTH...  33.7 us
    all_to_all x1, waiting for transfers between devices, local(): lax.all_to_all(widened, 'seq', split_axis=0, concat_axis=0, tiled=True)  23 us
    all_to_all x1, blocking collectives, local(): lax.all_to_all(highest_score, 'seq', split_axis=0, concat_axis=0, tiled=T...  13.7 us
  transfers between devices with their start and end apart: 4, of which 4 were waited for; matrix products, arithmetic and copies ran while one was open for 1% of the time, Pallas kernels for 0%

commit v1 on v0

--- a/solution.py
+++ b/solution.py
@@ -185,9 +185,14 @@
     cache_mine = lax.dynamic_slice_in_dim(prefix_slot_cache, first_shared, shared_heads, 2).reshape(
         cache_extent, shared_heads, pair_width
     )
-    query_all = lax.all_gather(
-        query_rows_all.reshape(rows_here, local_heads * HEAD_WIDTH), "seq", axis=0, tiled=True
-    )
+    vec = query_rows_all.reshape(rows_here, local_heads * HEAD_WIDTH)
+    local_now = lax.all_to_all(
+        jnp.stack([vec for _ in range(lax.axis_size("seq"))], axis=0),
+        axis_name="seq",
+        split_axis=0,
+        concat_axis=0,
+    )
+    query_all = jnp.concatenate(local_now, axis=0)
     query_all = query_all.reshape(all_tokens, shared_heads, query_per_head, HEAD_WIDTH)
     all_pos = jnp.arange(all_tokens, dtype=jnp.int32)
     all_req, all_pre, _ = token_tables(request_prefix, suffix_lengths, all_pos, prefix_length)

time: 404 us -> 395 us (0.978)
  blocking collectives: 47.4 us -> 13.8 us
  waiting for transfers between devices: 279 us -> 291 us
  starting transfers between devices: 9.69 us -> 21.3 us
    all_gather x1 -> x0, blocking collectives: 33.7 us -> none  [local(): lax.all_gather(query_rows_all.reshape(rows_here, local_heads * HEAD_WIDTH...]
    all_to_all x0 -> x1, waiting for transfers between devices: none -> 11.7 us  [local(): lax.all_to_all(jnp.stack([vec for _ in range(lax.axis_size('seq'))], axis...]
    all_to_all x0 -> x1, starting transfers between devices: none -> 11.6 us  [local(): lax.all_to_all(jnp.stack([vec for _ in range(lax.axis_size('seq'))], axis...]
  transfers between devices with their start and end apart: 4 -> 5, of which waited for: 4 -> 5; matrix products, arithmetic and copies ran while one was open for 1% -> 1% of each run, Pallas kernels for 0% -> 0%
where the time goes in v1:
time: 395 us; the launch traced here: 394 us
  waiting for transfers between devices  291 us (74%)
  other arithmetic  21.6 us (5%)
  starting transfers between devices  21.3 us (5%)
  matrix products  15.4 us (4%)
  between operations  14.5 us (4%)
  local copies, waits for them, and re-layouts  14.2 us (4%)
  blocking collectives  13.8 us (3%)
    psum x1, waiting for transfers between devices, local(): lax.psum(partial_out.astype(jnp.bfloat16), 'mp').astype(jnp.float32)  167 us
    unnamed x3, waiting for transfers between devices  82.9 us
    all_to_all x1, waiting for transfers between devices, local(): lax.all_to_all(widened, 'seq', split_axis=0, concat_axis=0, tiled=True)  22.9 us
    all_to_all x1, blocking collectives, local(): lax.all_to_all(highest_score, 'seq', split_axis=0, concat_axis=0, tiled=T...  13.8 us
    all_to_all x1, waiting for transfers between devices, local(): lax.all_to_all(jnp.stack([vec for _ in range(lax.axis_size('seq'))], axis...  11.7 us
    all_to_all x1, starting transfers between devices, local(): lax.all_to_all(jnp.stack([vec for _ in range(lax.axis_size('seq'))], axis...  11.6 us
  transfers between devices with their start and end apart: 5, of which 5 were waited for; matrix products, arithmetic and copies ran while one was open for 1% of the time, Pallas kernels for 0%

profile of v1, /device:TPU:8, one launch (start us, length us, event | category | flops | bytes accessed | tf_op | source)
XLA Modules:
  0.0 394.3 jit_solution(14254599207039932381)
XLA Ops:
  7.2 1.4 fusion.20
  8.6 0.7 copy.48
  9.6 0.7 sub.47
  10.3 1.8 convolution_convert_fusion.2
  12.3 0.4 multiply_reduce_fusion.1
  13.0 0.2 fusion.58
  13.3 0.9 stack.7
  14.2 11.6 %all-to-all-start = ((bf16[16,128,128]{2,1,0:T(8,128)(2,1)}), bf16[16,128,128]{2,1,0:T(8,128)(2,1)S(1)}, u32[]{:S(2)}, u32[]{:S(2)}) async-start(bf16[16,128,128]{2,1,0:T(8,128)(2,1)} %stack.7), calls=%async_computation | async-start | bytes 1048576 | tf_op jit(solution)/shard_map/all_to_all | solution.py:189
  26.0 0.2 select_reduce_fusion
  26.5 0.1 copy.61
  26.7 0.5 constant_dynamic-slice_fusion.3
  27.4 11.7 %all-to-all-done = bf16[16,128,128]{2,1,0:T(8,128)(2,1)S(1)} async-done(((bf16[16,128,128]{2,1,0:T(8,128)(2,1)}), bf16[16,128,128]{2,1,0:T(8,128)(2,1)S(1)}, u32[]{:S(2)}, u32[]{:S(2)}) %all-to-all-start) | async-done | bytes 524320 | tf_op jit(solution)/shard_map/all_to_all | solution.py:189
  39.1 33.2 %while.14 = (s32[]{:T(128)}, f32[4,512,1,1]{1,3,2,0:T(1,128)S(1)}, f32[4,512,1,1]{1,3,2,0:T(1,128)}, bf16[4,512,1,1,128]{4,1,3,2,0:T(8,128)(2,1)}, s32[640]{0:T(...) while((s32[]{:T(128)}, f32[4,512,1,1]{1,3,2,0:T(1,128)S(1)}, ...), condition=%wide.region_15.16_spmd, body=%wide.region_9.15_spmd.sunk | while | flops 172817920 | bytes 6144739 | solution.py:113
  39.1 1.0 fusion.76
  40.8 4.6 %conditional.2 = (f32[1,512,1,1]{1,3,2,0:T(1,128)}, f32[1,512,1,1]{1,3,2,0:T(1,128)}, bf16[1,512,1,1,128]{4,1,3,2,0:T(8,128)(2,1)S(1)}) conditional(s32[]{:T(128)} %convert_element_type.196, () %tuple.63, (pred[512,640]{1,0:T(32,128)(4,1)S(1)}, bf16[4,512,1,1,128]{4,1,3,2,0:T(8,128)(2,1)S(1)}, s32[]{:T(128)}, bf16[640,1,128]{2,0,1:T(8,128)(2,1)S(1)}, ...), branch_computations={%region_11.11_spmd, %region_12.14_spmd} | conditional | flops 170851840 | bytes 5519388 | solution.py:111
  40.9 1.1 fusion.66
  41.9 1.7 fusion.5
  43.7 0.7 broadcast_maximum_fusion
  44.3 1.1 fusion.3
  45.5 1.3 constant_dynamic-update-slice_fusion.5
  46.7 0.7 constant_dynamic-update-slice_fusion.6
  47.4 1.0 fusion.76
  49.1 4.6 %conditional.2 = (f32[1,512,1,1]{1,3,2,0:T(1,128)}, f32[1,512,1,1]{1,3,2,0:T(1,128)}, bf16[1,512,1,1,128]{4,1,3,2,0:T(8,128)(2,1)S(1)}) conditional(s32[]{:T(128)} %convert_element_type.196, () %tuple.63, (pred[512,640]{1,0:T(32,128)(4,1)S(1)}, bf16[4,512,1,1,128]{4,1,3,2,0:T(8,128)(2,1)S(1)}, s32[]{:T(128)}, bf16[640,1,128]{2,0,1:T(8,128)(2,1)S(1)}, ...), branch_computations={%region_11.11_spmd, %region_12.14_spmd} | conditional | flops 170851840 | bytes 5519388 | solution.py:111
  49.2 1.1 fusion.66
  50.2 1.7 fusion.5
  52.0 0.7 broadcast_maximum_fusion
  52.6 1.1 fusion.3
  53.8 1.3 constant_dynamic-update-slice_fusion.5
  55.0 0.7 constant_dynamic-update-slice_fusion.6
  55.7 1.0 fusion.76
  57.4 4.6 %conditional.2 = (f32[1,512,1,1]{1,3,2,0:T(1,128)}, f32[1,512,1,1]{1,3,2,0:T(1,128)}, bf16[1,512,1,1,128]{4,1,3,2,0:T(8,128)(2,1)S(1)}) conditional(s32[]{:T(128)} %convert_element_type.196, () %tuple.63, (pred[512,640]{1,0:T(32,128)(4,1)S(1)}, bf16[4,512,1,1,128]{4,1,3,2,0:T(8,128)(2,1)S(1)}, s32[]{:T(128)}, bf16[640,1,128]{2,0,1:T(8,128)(2,1)S(1)}, ...), branch_computations={%region_11.11_spmd, %region_12.14_spmd} | conditional | flops 170851840 | bytes 5519388 | solution.py:111
  57.5 1.1 fusion.66
  58.5 1.7 fusion.5
  60.3 0.7 broadcast_maximum_fusion
  60.9 1.1 fusion.3
  62.1 1.3 constant_dynamic-update-slice_fusion.5
  63.4 0.7 constant_dynamic-update-slice_fusion.6
  64.0 1.0 fusion.76
  65.7 4.6 %conditional.2 = (f32[1,512,1,1]{1,3,2,0:T(1,128)}, f32[1,512,1,1]{1,3,2,0:T(1,128)}, bf16[1,512,1,1,128]{4,1,3,2,0:T(8,128)(2,1)S(1)}) conditional(s32[]{:T(128)} %convert_element_type.196, () %tuple.63, (pred[512,640]{1,0:T(32,128)(4,1)S(1)}, bf16[4,512,1,1,128]{4,1,3,2,0:T(8,128)(2,1)S(1)}, s32[]{:T(128)}, bf16[640,1,128]{2,0,1:T(8,128)(2,1)S(1)}, ...), branch_computations={%region_11.11_spmd, %region_12.14_spmd} | conditional | flops 170851840 | bytes 5519388 | solution.py:111
  65.8 1.1 fusion.66
  66.8 1.7 fusion.5
  68.6 0.7 broadcast_maximum_fusion
  69.2 1.1 fusion.3
  70.4 1.3 constant_dynamic-update-slice_fusion.5
  71.7 0.7 constant_dynamic-update-slice_fusion.6
  72.3 13.8 %all_to_all.20 = f32[16,128,1,1]{1,3,2,0:T(1,128)S(1)} all-to-all(f32[16,128,1,1]{1,3,2,0:T(1,128)S(1)} %bitcast.117), channel_id=1, replica_groups=mesh['seq'=16,'mp'=16] {'seq'}, dimensions={0} | all-to-all | bytes 16384 | tf_op jit(solution)/shard_map/all_to_all | solution.py:223
  86.2 4.7 %all-to-all-start.1 = ((f32[16,128,1,1]{1,3,2,0:T(1,128)}), f32[16,128,1,1]{1,3,2,0:T(1,128)S(1)}, u32[]{:S(2)}, u32[]{:S(2)}) async-start(f32[16,128,1,1]{1,3,2,0:T(1,128)} %bitcast.30), calls=%async_computation.1 | async-start | bytes 16384 | tf_op jit(solution)/shard_map/all_to_all | solution.py:224
  90.9 2.1 convert_element_type.122
  93.0 6.5 %all-to-all-done.1 = f32[16,128,1,1]{1,3,2,0:T(1,128)S(1)} async-done(((f32[16,128,1,1]{1,3,2,0:T(1,128)}), f32[16,128,1,1]{1,3,2,0:T(1,128)S(1)}, u32[]{:S(2)}, u32[]{:S(2)}) %all-to-all-start.1) | async-done | bytes 8224 | tf_op jit(solution)/shard_map/all_to_all | solution.py:224
  99.5 4.9 %all-to-all-start.3 = ((f32[16,128,1,1,128]{4,1,3,2,0:T(8,128)}), f32[16,128,1,1,128]{4,1,3,2,0:T(8,128)S(1)}, u32[]{:S(2)}, u32[]{:S(2)}) async-start(f32[16,128,1,1,128]{4,1,3,2,0:T(8,128)} %convert_element_type.122), calls=%async_computation.3 | async-start | bytes 2097152 | tf_op jit(solution)/shard_map/all_to_all | solution.py:222
  104.5 22.9 %all-to-all-done.3 = f32[16,128,1,1,128]{4,1,3,2,0:T(8,128)S(1)} async-done(((f32[16,128,1,1,128]{4,1,3,2,0:T(8,128)}), f32[16,128,1,1,128]{4,1,3,2,0:T(8,128)S(1)}, u32[]{:S(2)}, u32[]{:S(2)}) %all-to-all-start.3) | async-done | bytes 1048608 | tf_op jit(solution)/shard_map/all_to_all | solution.py:222
  127.4 0.3 multiply_reduce_fusion
  127.8 0.7 copy-done.3
  128.5 1.2 convolution_convert_fusion.1
  129.7 166.8 %all-reduce.5.cloned.1.call-done = bf16[128,2048]{1,0:T(8,128)(2,1)} async-done(((bf16[128,2048]{1,0:T(8,128)(2,1)}), bf16[128,2048]{1,0:T(8,128)(2,1)}) %all-reduce.5.cloned.1.call-update) | async-done | bytes 524304 | tf_op jit(solution)/shard_map/psum | solution.py:234
  296.5 1.4 fusion.17
  298.0 0.1 copy-done.7
  298.1 0.5 fusion.32
  298.6 2.8 convolution_convert_fusion
  301.4 1.0 copy.58
  302.4 0.7 copy.63
  303.1 82.8 %reduce-scatter.4.cloned.1.call-done = bf16[128,128]{1,0:T(8,128)(2,1)} async-done(((bf16[2048,128]{1,0:T(8,128)(2,1)}), bf16[128,128]{1,0:T(8,128)(2,1)}) %reduce-scatter.4.cloned.1.call-update) | async-done | bytes 32784
  386.0 0.9 copy.59
  386.9 0.6 add_convert_fusion
  (78 shorter events, 1.6 us)
Async XLA Ops:
  7.2 19.5 %copy-start = (bf16[2,256,8,256]{3,2,1,0:T(8,128)(2,1)S(1)}, bf16[2,256,8,256]{3,2,1,0:T(8,128)(2,1)}, u32[]{:S(2)}) copy-start(bf16[2,256,8,256]{3,2,1,0:T(8,128)(2,1)} %param.30) | copy-start | bytes 6291460
  7.2 5.1 %copy-start.1 = (bf16[128,2048]{1,0:T(8,128)(2,1)S(1)}, bf16[128,2048]{1,0:T(8,128)(2,1)}, u32[]{:S(2)}) copy-start(bf16[128,2048]{1,0:T(8,128)(2,1)} %param.19) | copy-start | bytes 1572868
  7.2 5.1 %copy-start.8 = (bf16[2048,128]{1,0:T(8,128)(2,1)S(1)}, bf16[2048,128]{1,0:T(8,128)(2,1)}, u32[]{:S(2)}) copy-start(bf16[2048,128]{1,0:T(8,128)(2,1)} %param.21) | copy-start | bytes 1572868
  7.2 5.1 %copy-start.9 = (f32[2048]{0:T(1024)S(1)}, f32[2048]{0:T(1024)}, u32[]{:S(2)}) copy-start(f32[2048]{0:T(1024)} %param.20) | copy-start | bytes 24580
  10.3 2.4 copy-start.4
  10.3 2.5 copy-start.5
  12.7 13.0 %copy-start.11 = (s32[32]{0:T(128)S(1)}, s32[32]{0:T(128)}, u32[]{:S(2)}) copy-start(s32[32]{0:T(128)} %param.31) | copy-start | bytes 388
  12.7 13.3 %copy-start.6 = (s32[32]{0:T(128)S(1)}, s32[32]{0:T(128)}, u32[]{:S(2)}) copy-start(s32[32]{0:T(128)} %param.32) | copy-start | bytes 388
  14.2 24.9 %all-to-all-start = ((bf16[16,128,128]{2,1,0:T(8,128)(2,1)}), bf16[16,128,128]{2,1,0:T(8,128)(2,1)S(1)}, u32[]{:S(2)}, u32[]{:S(2)}) async-start(bf16[16,128,128]{2,1,0:T(8,128)(2,1)} %stack.7), calls=%async_computation | async-start | bytes 1048576 | tf_op jit(solution)/shard_map/all_to_all | solution.py:189
  86.2 13.3 %all-to-all-start.1 = ((f32[16,128,1,1]{1,3,2,0:T(1,128)}), f32[16,128,1,1]{1,3,2,0:T(1,128)S(1)}, u32[]{:S(2)}, u32[]{:S(2)}) async-start(f32[16,128,1,1]{1,3,2,0:T(1,128)} %bitcast.30), calls=%async_computation.1 | async-start | bytes 16384 | tf_op jit(solution)/shard_map/all_to_all | solution.py:224
  99.5 27.9 %all-to-all-start.3 = ((f32[16,128,1,1,128]{4,1,3,2,0:T(8,128)}), f32[16,128,1,1,128]{4,1,3,2,0:T(8,128)S(1)}, u32[]{:S(2)}, u32[]{:S(2)}) async-start(f32[16,128,1,1,128]{4,1,3,2,0:T(8,128)} %convert_element_type.122), calls=%async_computation.3 | async-start | bytes 2097152 | tf_op jit(solution)/shard_map/all_to_all | solution.py:222
  104.4 192.1 %all-reduce.5.cloned.1.call-start = ((), (), s32[]{:S(2)}) async-start(), calls=%async_computation.5 | async-start | bytes 1048576 | tf_op jit(solution)/shard_map/psum | solution.py:234
  127.4 1.0 copy-start.3
  127.8 168.8 %copy-start.2 = (bf16[128,2048]{1,0:T(8,128)(2,1)S(1)}, bf16[128,2048]{1,0:T(8,128)(2,1)}, u32[]{:S(2)}) copy-start(bf16[128,2048]{1,0:T(8,128)(2,1)} %param.19) | copy-start | bytes 1572868
  129.6 168.3 %copy-start.10 = (f32[2048]{0:T(1024)S(1)}, f32[2048]{0:T(1024)}, u32[]{:S(2)}) copy-start(f32[2048]{0:T(1024)} %param.26) | copy-start | bytes 24580
  129.7 256.3 %reduce-scatter.4.cloned.1.call-start = ((), (), s32[]{:S(2)}) async-start(), calls=%async_computation.6 | async-start | bytes 557056
  296.5 1.6 copy-start.7
Sparse Core Ops, SparseCore 0:
  129.8 166.6 all-reduce.4
  302.5 83.4 reduce-scatter.3
